TPU v7x, 32 devices: a whole 2x2x4 slice. The times are simulated.
32 devices in a mesh: vol: 2 (over core), wide: 8 (over z, x), narrow: 2 (over y).
Axes of the slice: x: 2, y: 2, z: 4, core: 2. Of those that a mesh axis runs over, the one named last changes fastest.
Arguments:
- forcing: float32 [2, 4, 384, 1024], P(None, 'vol', 'narrow', 'wide'), may hold values from -180 to 180
- material_ids: int32 [4, 384, 1024], P('vol', 'narrow', 'wide'), may hold values from 0 to 7
- materials: float32 [8], replicated, may hold values from 0.5 to 2
- boundary_operator: bfloat16 [1024, 32768], P('wide', 'narrow'), may hold values from -0.03125 to 0.03125
Outputs:
- pressure: float32 [2, 4, 384, 1024], P(None, 'vol', 'narrow', 'wide')
- traction: float32 [1024, 2], P(('wide', 'narrow'), 'vol')
All inputs are finite; a program needn't handle non-finite values.
Results may differ from a plain program's by a relative error of at most 0.0031.
Values may be sent and summed in bfloat16 or wider, within the bound.
No kernel may reach another device: no remote copies, remote signals or barrier semaphores. Data moves between devices by JAX's collectives and lax.ppermute only.
A program may use at most 128 MiB of HBM per device.

v0:
```python
import jax
import jax.numpy as jnp
from jax import lax
from jax.sharding import PartitionSpec as P

BY = 16
RY = 1
RX = 64
MAT = 8
ITERS = 2
lower_edge = 0.25
upper_edge = 1.75
mass_ratio = 26.0
couple_gain = 40.0


def with_halo(shard, sides, width):
    for axis, dim in sides:
        peers, length = (lax.axis_size(axis), shard.shape[dim])
        up = [(i, (i + 1) % peers) for i in range(peers - 1)]
        down = [(j, i) for i, j in up]
        last = lax.slice_in_dim(shard, length - width, length, axis=dim)
        first = lax.slice_in_dim(shard, 0, width, axis=dim)
        before = lax.ppermute(last, axis, up)
        after = lax.ppermute(first, axis, down)
        shard = jnp.concatenate([before, shard, after], axis=dim)
    return shard


def from_root(shard, axis, root):
    mine = lax.axis_index(axis) == root
    return lax.psum(jnp.where(mine, shard, jnp.zeros_like(shard)), axis)


def sweep_weights():
    middle = (upper_edge + lower_edge) / 2.0
    spread = (upper_edge - lower_edge) / 2.0
    center_ratio = middle / spread
    ratio_last = 1.0 / center_ratio
    weights = [(0.0, 1.0 / middle)]
    ratio_next = 1.0 / (2.0 * center_ratio - ratio_last)
    weights.append((ratio_next * ratio_last, 2.0 * ratio_next / spread))
    return weights


def box_sum(padded):
    along = padded[..., :-2] + padded[..., 1:-1] + padded[..., 2:]
    along = along[..., :-2, :] + along[..., 1:-1, :] + along[..., 2:, :]
    return along[..., :-2, :, :] + along[..., 1:-1, :, :] + along[..., 2:, :, :]


def apply_operator(padded, center, cond_pad, conductance, diagonal):
    neighbours = box_sum(padded) - center
    weighted = box_sum(padded * cond_pad) - conductance * center
    return diagonal * center - 0.5 * (conductance * neighbours + weighted)


def relax(vol_field, source, cond_pad, conductance, diagonal):
    moved = jnp.zeros_like(vol_field)
    for keep_weight, gain_weight in sweep_weights():
        padded = with_halo(vol_field, (("vol", 1), ("wide", 3), ("narrow", 2)), 1)
        scaled = (
            source - apply_operator(padded, vol_field, cond_pad, conductance, diagonal)
        ) / diagonal
        moved = keep_weight * moved + gain_weight * scaled
        vol_field = vol_field + moved
    return vol_field


def fold_traces(mine, plane):
    return jnp.einsum(
        "ryx,kyx->rk",
        plane,
        lax.all_gather(mine, "wide", axis=2, tiled=True),
        preferred_element_type=jnp.float32,
    )


def local(forcing, material_ids, materials, boundary_operator):
    conductance = jnp.zeros(material_ids.shape, jnp.float32)
    for number in range(MAT):
        conductance = conductance + jnp.where(material_ids == number, materials[number], 0.0)
    cond_pad = with_halo(conductance, (("vol", 0), ("wide", 2), ("narrow", 1)), 1)
    diagonal = (
        0.5 * (26.0 * conductance + (box_sum(cond_pad) - conductance)) + mass_ratio * conductance
    )
    vol_count = lax.axis_size("vol")
    last_vol = vol_count - 1
    own_vol = lax.axis_index("vol")
    excite = forcing.shape[0]
    half_count = excite // vol_count
    tile_rows = boundary_operator.shape[0]
    cells_y = forcing.shape[2]
    cells_x = forcing.shape[3]
    stride = cells_y // BY
    plane = boundary_operator.reshape(tile_rows, BY, -1)
    is_top = (own_vol == last_vol).astype(jnp.float32)
    pressure = jnp.zeros(forcing.shape, jnp.float32)
    source = forcing
    traction = jnp.zeros((tile_rows // lax.axis_size("narrow"), half_count), jnp.float32)
    for outer in range(ITERS):
        pressure = relax(pressure, source, cond_pad, conductance, diagonal)
        surface = pressure[:, -1, ::stride].astype(jnp.bfloat16)
        copied = from_root(surface, "vol", last_vol)
        mine = lax.dynamic_slice_in_dim(copied, own_vol * half_count, half_count, 0)
        partial_rows = fold_traces(mine, plane)
        summed = lax.psum(partial_rows, "narrow")
        share = summed.shape[0] // lax.axis_size("narrow")
        traction = lax.dynamic_slice_in_dim(summed, lax.axis_index("narrow") * share, share, 0)
        if outer + 1 < ITERS:
            shared = lax.all_gather(traction, "vol", axis=1, tiled=True)
            placed = jnp.transpose(shared).reshape(excite, RY, RX)
            placed = jnp.pad(placed, ((0, 0), (0, cells_y - RY), (0, cells_x - RX)))
            source = forcing.at[:, -1].add(couple_gain * is_top * placed)
    return (pressure, traction)


def solution(mesh):
    placed = (
        P(None, "vol", "narrow", "wide"),
        P("vol", "narrow", "wide"),
        P(),
        P("wide", "narrow"),
    )
    return jax.shard_map(
        local,
        mesh=mesh,
        in_specs=placed,
        out_specs=(P(None, "vol", "narrow", "wide"), P(("wide", "narrow"), "vol")),
        check_vma=False,
    )
```

profile of v0, /device:TPU:0, one launch (start us, length us, event | category | flops | bytes accessed | tf_op | source)
XLA Modules:
  0.0 236.0 jit_solution(11555738974021824176)
XLA Ops:
  2.3 6.8 %broadcast_multiply_fusion.5 = (f32[2,192,128]{2,1,0:T(8,128)}, f32[2,192,128]{2,1,0:T(8,128)S(1)}) fusion(f32[]{:T(128)} %bitcast.7, s32[2,192,128]{2,1,0:T(8,128)} %param.7, f32[]{:T(128)} %bitcast.6, f32[]{:T(128)} %bitcast.5, f32[]{:T(128)} %bitcast.4, f32[]{:T(128)} %bitcast.3, f32[]{:T(128)} %bitcast.2, f32[]{:T(128)} %bitcast.1, f32[]{:T(128)} %bitcast), kind=kLoop, calls=%fused_computation.111 | loop fusion | flops 1179648 | bytes 589856 | tf_op jit(solution)/shard_map/mul | solution.py:54
  9.1 2.4 %collective-permute-start = (f32[1,192,128]{2,1,0:T(8,128)S(1)}, f32[1,192,128]{2,1,0:T(8,128)S(1)}, u32[]{:S(2)}, u32[]{:S(2)}) collective-permute-start(f32[1,192,128]{2,1,0:T(8,128)S(1)} %get-tuple-element.64), channel_id=1, source_target_pairs={{0,16},{1,17},{2,18},{3,19},{4,20},{5,21},{6,22},{7,23},{8,24},{9,... | collective-permute-start | bytes 294920 | tf_op jit(solution)/shard_map/ppermute | solution.py:24
  12.8 1.9 collective-permute-done.1
  14.9 4.2 %collective-permute-start.2 = (f32[4,192,1]{2,1,0:T(8,128)S(1)}, f32[4,192,1]{2,1,0:T(8,128)S(1)}, u32[]{:S(2)}, u32[]{:S(2)}) collective-permute-start(f32[4,192,1]{2,1,0:T(8,128)S(1)} %get-tuple-element.62), channel_id=1, source_target_pairs={{0,2},{2,4},{4,6},{6,8},{8,10},{10,12},{12,14},{1,3},{3,5},{5,7},{... | collective-permute-start | bytes 9224 | tf_op jit(solution)/shard_map/ppermute | solution.py:24
  20.5 15.8 %collective-permute-done.2 = f32[4,192,1]{2,1,0:T(8,128)S(1)} collective-permute-done((f32[4,192,1]{2,1,0:T(8,128)S(1)}, f32[4,192,1]{2,1,0:T(8,128)S(1)}, u32[]{:S(2)}, u32[]{:S(2)}) %collective-permute-start.2) | collective-permute-done | bytes 3104 | tf_op jit(solution)/shard_map/ppermute | solution.py:24
  36.3 3.4 %collective-permute-start.4 = (f32[4,1,130]{2,1,0:T(1,128)S(1)}, f32[4,1,130]{2,1,0:T(1,128)S(1)}, u32[]{:S(2)}, u32[]{:S(2)}) collective-permute-start(f32[4,1,130]{2,1,0:T(1,128)S(1)} %get-tuple-element.44), channel_id=1, source_target_pairs={{0,1},{2,3},{4,5},{6,7},{8,9},{10,11},{12,13},{14,15},{16,17},{18,... | collective-permute-start | bytes 6248 | tf_op jit(solution)/shard_map/ppermute | solution.py:24
  42.4 3.0 %collective-permute-start.6 = (f32[2,1,192,128]{3,2,0,1:T(8,128)S(1)}, f32[2,1,192,128]{3,2,0,1:T(8,128)S(1)}, u32[]{:S(2)}, u32[]{:S(2)}) collective-permute-start(f32[2,1,192,128]{3,2,0,1:T(8,128)S(1)} %broadcast.51), channel_id=1, source_target_pairs={{0,16},{1,17},{2,18},{3,19},{4,20},{5,21},{6,22},{7,23},{8,24},{9,... | collective-permute-start | bytes 589832 | tf_op jit(solution)/shard_map/ppermute | solution.py:24
  50.9 5.0 %collective-permute-start.8 = (f32[2,4,192,1]{2,1,3,0:T(4,128)S(1)}, f32[2,4,192,1]{2,1,3,0:T(4,128)S(1)}, u32[]{:S(2)}, u32[]{:S(2)}) collective-permute-start(f32[2,4,192,1]{2,1,3,0:T(4,128)S(1)} %copy.19), channel_id=1, source_target_pairs={{0,2},{2,4},{4,6},{6,8},{8,10},{10,12},{12,14},{1,3},{3,5},{5,7},{... | collective-permute-start | bytes 18440 | tf_op jit(solution)/shard_map/ppermute | solution.py:24
  58.0 4.5 %collective-permute-start.10 = (f32[2,4,1,130]{3,2,0,1:T(1,128)S(1)}, f32[2,4,1,130]{3,2,0,1:T(1,128)S(1)}, u32[]{:S(2)}, u32[]{:S(2)}) collective-permute-start(f32[2,4,1,130]{3,2,0,1:T(1,128)S(1)} %get-tuple-element.42), channel_id=1, source_target_pairs={{0,1},{2,3},{4,5},{6,7},{8,9},{10,11},{12,13},{14,15},{16,17},{18,... | collective-permute-start | bytes 12488 | tf_op jit(solution)/shard_map/ppermute | solution.py:24
  65.1 3.0 %collective-permute-done.11 = f32[2,4,1,130]{3,2,0,1:T(1,128)S(1)} collective-permute-done((f32[2,4,1,130]{3,2,0,1:T(1,128)S(1)}, f32[2,4,1,130]{3,2,0,1:T(1,128)S(1)}, u32[]{:S(2)}, u32[]{:S(2)}) %collective-permute-start.11) | collective-permute-done | bytes 4192 | tf_op jit(solution)/shard_map/ppermute | solution.py:25
  68.1 1.6 broadcast_multiply_fusion.3
  75.5 2.0 collective-permute-done.13
  78.8 4.8 %collective-permute-start.14 = (f32[2,4,192,1]{2,1,3,0:T(4,128)S(1)}, f32[2,4,192,1]{2,1,3,0:T(4,128)S(1)}, u32[]{:S(2)}, u32[]{:S(2)}) collective-permute-start(f32[2,4,192,1]{2,1,3,0:T(4,128)S(1)} %copy.24), channel_id=1, source_target_pairs={{0,2},{2,4},{4,6},{6,8},{8,10},{10,12},{12,14},{1,3},{3,5},{5,7},{... | collective-permute-start | bytes 18440 | tf_op jit(solution)/shard_map/ppermute | solution.py:24
  85.6 5.1 %collective-permute-done.15 = f32[2,4,192,1]{2,1,3,0:T(4,128)S(1)} collective-permute-done((f32[2,4,192,1]{2,1,3,0:T(4,128)S(1)}, f32[2,4,192,1]{2,1,3,0:T(4,128)S(1)}, u32[]{:S(2)}, u32[]{:S(2)}) %collective-permute-start.15) | collective-permute-done | bytes 6176 | tf_op jit(solution)/shard_map/ppermute | solution.py:25
  94.8 6.4 %copy.43 = bf16[128,16384]{0,1:T(8,128)(2,1)} copy(bf16[128,16384]{1,0:T(8,128)(2,1)} %param.9) | data formatting | bytes 8388608 | tf_op jit(solution)/shard_map/reshape | solution.py:96
  101.2 1.7 broadcast_multiply_fusion.2
  105.4 2.5 %psum.28 = bf16[2,16,128]{2,1,0:T(8,128)(2,1)S(1)} all-reduce(bf16[2,16,128]{2,1,0:T(8,128)(2,1)S(1)} %select_bitcast_fusion.1), channel_id=1, replica_groups=mesh['vol'=2,'wide'=8,'narrow'=2] {'vol'}, use_global_device_ids=true, to_apply=%region_0.1 | all-reduce | flops 4096 | bytes 16384 | tf_op jit(solution)/shard_map/psum | solution.py:32
  107.9 26.0 %all_gather.9 = bf16[1,16,1024]{2,1,0:T(8,128)(2,1)S(1)} all-gather(bf16[1,16,128]{2,1,0:T(8,128)(2,1)S(1)} %constant_dynamic-slice_fusion.3), channel_id=1, replica_groups=mesh['vol'=2,'wide'=8,'narrow'=2] {'wide'}, dimensions={2}, use_global_device_ids=true | all-gather | bytes 36864 | tf_op jit(solution)/shard_map/all_gather | solution.py:74
  136.6 2.9 %convolution_bitcast_fusion.1 = f32[128,1]{0,1:T(1,128)S(1)} fusion(bf16[128,16,1024]{0,2,1:T(8,128)(2,1)} %bitcast.31, bf16[16,1024,1]{1,0,2:T(8,128)(2,1)S(1)} %bitcast.33), kind=kOutput, calls=%fused_computation.5 | convolution fusion | flops 4194304 | bytes 4227584 | tf_op jit(solution)/shard_map/ryx,kyx->rk/dot_general | solution.py:71
  139.4 5.5 %psum.29 = f32[128,1]{0,1:T(1,128)S(1)} all-reduce(f32[128,1]{0,1:T(1,128)S(1)} %convolution_bitcast_fusion.1), channel_id=1, replica_groups=mesh['vol'=2,'wide'=8,'narrow'=2] {'narrow'}, use_global_device_ids=true, to_apply=%region_1.2 | all-reduce | flops 128 | bytes 1024 | tf_op jit(solution)/shard_map/psum | solution.py:107
  147.7 4.5 %collective-permute-start.20 = (f32[2,4,192,1]{2,1,3,0:T(4,128)S(1)}, f32[2,4,192,1]{2,1,3,0:T(4,128)S(1)}, u32[]{:S(2)}, u32[]{:S(2)}) collective-permute-start(f32[2,4,192,1]{2,1,3,0:T(4,128)S(1)} %copy.31), channel_id=1, source_target_pairs={{0,2},{2,4},{4,6},{6,8},{8,10},{10,12},{12,14},{1,3},{3,5},{5,7},{... | collective-permute-start | bytes 18440 | tf_op jit(solution)/shard_map/ppermute | solution.py:24
  152.4 1.8 all-gather
  155.7 3.9 %collective-permute-start.22 = (f32[2,4,1,130]{3,2,0,1:T(1,128)S(1)}, f32[2,4,1,130]{3,2,0,1:T(1,128)S(1)}, u32[]{:S(2)}, u32[]{:S(2)}) collective-permute-start(f32[2,4,1,130]{3,2,0,1:T(1,128)S(1)} %get-tuple-element.38), channel_id=1, source_target_pairs={{0,1},{2,3},{4,5},{6,7},{8,9},{10,11},{12,13},{14,15},{16,17},{18,... | collective-permute-start | bytes 12488 | tf_op jit(solution)/shard_map/ppermute | solution.py:24
  161.1 4.2 %collective-permute-done.23 = f32[2,4,1,130]{3,2,0,1:T(1,128)S(1)} collective-permute-done((f32[2,4,1,130]{3,2,0,1:T(1,128)S(1)}, f32[2,4,1,130]{3,2,0,1:T(1,128)S(1)}, u32[]{:S(2)}, u32[]{:S(2)}) %collective-permute-start.23) | collective-permute-done | bytes 4192 | tf_op jit(solution)/shard_map/ppermute | solution.py:25
  171.9 2.0 collective-permute-done.25
  175.3 4.8 %collective-permute-start.26 = (f32[2,4,192,1]{2,1,3,0:T(4,128)S(1)}, f32[2,4,192,1]{2,1,3,0:T(4,128)S(1)}, u32[]{:S(2)}, u32[]{:S(2)}) collective-permute-start(f32[2,4,192,1]{2,1,3,0:T(4,128)S(1)} %copy.35), channel_id=1, source_target_pairs={{0,2},{2,4},{4,6},{6,8},{8,10},{10,12},{12,14},{1,3},{3,5},{5,7},{... | collective-permute-start | bytes 18440 | tf_op jit(solution)/shard_map/ppermute | solution.py:24
  182.0 4.6 %collective-permute-done.27 = f32[2,4,192,1]{2,1,3,0:T(4,128)S(1)} collective-permute-done((f32[2,4,192,1]{2,1,3,0:T(4,128)S(1)}, f32[2,4,192,1]{2,1,3,0:T(4,128)S(1)}, u32[]{:S(2)}, u32[]{:S(2)}) %collective-permute-start.27) | collective-permute-done | bytes 6176 | tf_op jit(solution)/shard_map/ppermute | solution.py:25
  190.8 4.2 %collective-permute-done.29 = f32[2,4,1,130]{3,2,0,1:T(1,128)S(1)} collective-permute-done((f32[2,4,1,130]{3,2,0,1:T(1,128)S(1)}, f32[2,4,1,130]{3,2,0,1:T(1,128)S(1)}, u32[]{:S(2)}, u32[]{:S(2)}) %collective-permute-start.29) | collective-permute-done | bytes 4192 | tf_op jit(solution)/shard_map/ppermute | solution.py:25
  198.3 2.5 %psum.30 = bf16[2,16,128]{2,1,0:T(8,128)(2,1)S(1)} all-reduce(bf16[2,16,128]{2,1,0:T(8,128)(2,1)S(1)} %select_bitcast_fusion), channel_id=1, replica_groups=mesh['vol'=2,'wide'=8,'narrow'=2] {'vol'}, use_global_device_ids=true, to_apply=%region_2.3 | all-reduce | flops 4096 | bytes 16384 | tf_op jit(solution)/shard_map/psum | solution.py:32
  200.8 26.0 %all_gather.11 = bf16[1,16,1024]{2,1,0:T(8,128)(2,1)S(1)} all-gather(bf16[1,16,128]{2,1,0:T(8,128)(2,1)S(1)} %constant_dynamic-slice_fusion.1), channel_id=1, replica_groups=mesh['vol'=2,'wide'=8,'narrow'=2] {'wide'}, dimensions={2}, use_global_device_ids=true | all-gather | bytes 36864 | tf_op jit(solution)/shard_map/all_gather | solution.py:74
  226.8 2.9 %convolution_bitcast_fusion = f32[128,1]{0,1:T(1,128)S(1)} fusion(bf16[128,16,1024]{0,2,1:T(8,128)(2,1)} %bitcast.32, bf16[16,1024,1]{1,0,2:T(8,128)(2,1)S(1)} %bitcast.34), kind=kOutput, calls=%fused_computation.4 | convolution fusion | flops 4194304 | bytes 4227584 | tf_op jit(solution)/shard_map/ryx,kyx->rk/dot_general | solution.py:71
  229.7 4.9 %psum.31 = f32[128,1]{0,1:T(1,128)S(1)} all-reduce(f32[128,1]{0,1:T(1,128)S(1)} %convolution_bitcast_fusion), channel_id=1, replica_groups=mesh['vol'=2,'wide'=8,'narrow'=2] {'narrow'}, use_global_device_ids=true, to_apply=%region_3.4 | all-reduce | flops 128 | bytes 1024 | tf_op jit(solution)/shard_map/psum | solution.py:107
  (150 shorter events, 59.4 us)
Async XLA Ops:
  9.1 3.7 %collective-permute-start = (f32[1,192,128]{2,1,0:T(8,128)S(1)}, f32[1,192,128]{2,1,0:T(8,128)S(1)}, u32[]{:S(2)}, u32[]{:S(2)}) collective-permute-start(f32[1,192,128]{2,1,0:T(8,128)S(1)} %get-tuple-element.64), channel_id=1, source_target_pairs={{0,16},{1,17},{2,18},{3,19},{4,20},{5,21},{6,22},{7,23},{8,24},{9,... | collective-permute-start | bytes 294920 | tf_op jit(solution)/shard_map/ppermute | solution.py:24
  11.5 3.2 %collective-permute-start.1 = (f32[1,192,128]{2,1,0:T(8,128)S(1)}, f32[1,192,128]{2,1,0:T(8,128)S(1)}, u32[]{:S(2)}, u32[]{:S(2)}) collective-permute-start(f32[1,192,128]{2,1,0:T(8,128)S(1)} %get-tuple-element.65), channel_id=1, source_target_pairs={{16,0},{17,1},{18,2},{19,3},{20,4},{21,5},{22,6},{23,7},{24,8},{25... | collective-permute-start | bytes 294920 | tf_op jit(solution)/shard_map/ppermute | solution.py:25
  14.9 21.3 %collective-permute-start.2 = (f32[4,192,1]{2,1,0:T(8,128)S(1)}, f32[4,192,1]{2,1,0:T(8,128)S(1)}, u32[]{:S(2)}, u32[]{:S(2)}) collective-permute-start(f32[4,192,1]{2,1,0:T(8,128)S(1)} %get-tuple-element.62), channel_id=1, source_target_pairs={{0,2},{2,4},{4,6},{6,8},{8,10},{10,12},{12,14},{1,3},{3,5},{5,7},{... | collective-permute-start | bytes 9224 | tf_op jit(solution)/shard_map/ppermute | solution.py:24
  19.2 17.1 %collective-permute-start.3 = (f32[4,192,1]{2,1,0:T(8,128)S(1)}, f32[4,192,1]{2,1,0:T(8,128)S(1)}, u32[]{:S(2)}, u32[]{:S(2)}) collective-permute-start(f32[4,192,1]{2,1,0:T(8,128)S(1)} %get-tuple-element.63), channel_id=1, source_target_pairs={{2,0},{4,2},{6,4},{8,6},{10,8},{12,10},{14,12},{3,1},{5,3},{7,5},{... | collective-permute-start | bytes 9224 | tf_op jit(solution)/shard_map/ppermute | solution.py:25
  36.3 9.1 %collective-permute-start.4 = (f32[4,1,130]{2,1,0:T(1,128)S(1)}, f32[4,1,130]{2,1,0:T(1,128)S(1)}, u32[]{:S(2)}, u32[]{:S(2)}) collective-permute-start(f32[4,1,130]{2,1,0:T(1,128)S(1)} %get-tuple-element.44), channel_id=1, source_target_pairs={{0,1},{2,3},{4,5},{6,7},{8,9},{10,11},{12,13},{14,15},{16,17},{18,... | collective-permute-start | bytes 6248 | tf_op jit(solution)/shard_map/ppermute | solution.py:24
  39.8 5.7 %collective-permute-start.5 = (f32[4,1,130]{2,1,0:T(1,128)S(1)}, f32[4,1,130]{2,1,0:T(1,128)S(1)}, u32[]{:S(2)}, u32[]{:S(2)}) collective-permute-start(f32[4,1,130]{2,1,0:T(1,128)S(1)} %get-tuple-element.45), channel_id=1, source_target_pairs={{1,0},{3,2},{5,4},{7,6},{9,8},{11,10},{13,12},{15,14},{17,16},{19,... | collective-permute-start | bytes 6248 | tf_op jit(solution)/shard_map/ppermute | solution.py:25
  41.1 5.1 %collective-permute-start.7 = (f32[2,1,192,128]{3,2,0,1:T(8,128)S(1)}, f32[2,1,192,128]{3,2,0,1:T(8,128)S(1)}, u32[]{:S(2)}, u32[]{:S(2)}) collective-permute-start(f32[2,1,192,128]{3,2,0,1:T(8,128)S(1)} %broadcast.51), channel_id=1, source_target_pairs={{16,0},{17,1},{18,2},{19,3},{20,4},{21,5},{22,6},{23,7},{24,8},{25... | collective-permute-start | bytes 589832 | tf_op jit(solution)/shard_map/ppermute | solution.py:25
  42.4 4.1 %collective-permute-start.6 = (f32[2,1,192,128]{3,2,0,1:T(8,128)S(1)}, f32[2,1,192,128]{3,2,0,1:T(8,128)S(1)}, u32[]{:S(2)}, u32[]{:S(2)}) collective-permute-start(f32[2,1,192,128]{3,2,0,1:T(8,128)S(1)} %broadcast.51), channel_id=1, source_target_pairs={{0,16},{1,17},{2,18},{3,19},{4,20},{5,21},{6,22},{7,23},{8,24},{9,... | collective-permute-start | bytes 589832 | tf_op jit(solution)/shard_map/ppermute | solution.py:24
  46.5 11.4 %copy-start.7 = (f32[2,1,192,128]{3,2,0,1:T(8,128)}, f32[2,1,192,128]{3,2,0,1:T(8,128)S(1)}, u32[]{:S(2)}) copy-start(f32[2,1,192,128]{3,2,0,1:T(8,128)S(1)} %collective-permute-done.6) | copy-start | bytes 589828
  49.6 8.0 %collective-permute-start.9 = (f32[2,4,192,1]{2,1,3,0:T(4,128)S(1)}, f32[2,4,192,1]{2,1,3,0:T(4,128)S(1)}, u32[]{:S(2)}, u32[]{:S(2)}) collective-permute-start(f32[2,4,192,1]{2,1,3,0:T(4,128)S(1)} %copy.20), channel_id=1, source_target_pairs={{2,0},{4,2},{6,4},{8,6},{10,8},{12,10},{14,12},{3,1},{5,3},{7,5},{... | collective-permute-start | bytes 18440 | tf_op jit(solution)/shard_map/ppermute | solution.py:25
  50.9 6.4 %collective-permute-start.8 = (f32[2,4,192,1]{2,1,3,0:T(4,128)S(1)}, f32[2,4,192,1]{2,1,3,0:T(4,128)S(1)}, u32[]{:S(2)}, u32[]{:S(2)}) collective-permute-start(f32[2,4,192,1]{2,1,3,0:T(4,128)S(1)} %copy.19), channel_id=1, source_target_pairs={{0,2},{2,4},{4,6},{6,8},{8,10},{10,12},{12,14},{1,3},{3,5},{5,7},{... | collective-permute-start | bytes 18440 | tf_op jit(solution)/shard_map/ppermute | solution.py:24
  58.0 7.0 %collective-permute-start.10 = (f32[2,4,1,130]{3,2,0,1:T(1,128)S(1)}, f32[2,4,1,130]{3,2,0,1:T(1,128)S(1)}, u32[]{:S(2)}, u32[]{:S(2)}) collective-permute-start(f32[2,4,1,130]{3,2,0,1:T(1,128)S(1)} %get-tuple-element.42), channel_id=1, source_target_pairs={{0,1},{2,3},{4,5},{6,7},{8,9},{10,11},{12,13},{14,15},{16,17},{18,... | collective-permute-start | bytes 12488 | tf_op jit(solution)/shard_map/ppermute | solution.py:24
  62.6 5.5 %collective-permute-start.11 = (f32[2,4,1,130]{3,2,0,1:T(1,128)S(1)}, f32[2,4,1,130]{3,2,0,1:T(1,128)S(1)}, u32[]{:S(2)}, u32[]{:S(2)}) collective-permute-start(f32[2,4,1,130]{3,2,0,1:T(1,128)S(1)} %get-tuple-element.43), channel_id=1, source_target_pairs={{1,0},{3,2},{5,4},{7,6},{9,8},{11,10},{13,12},{15,14},{17,16},{19,... | collective-permute-start | bytes 12488 | tf_op jit(solution)/shard_map/ppermute | solution.py:25
  65.1 39.2 %copy-start = (f32[2,192,128]{2,1,0:T(8,128)}, f32[2,192,128]{2,1,0:T(8,128)S(1)}, u32[]{:S(2)}) copy-start(f32[2,192,128]{2,1,0:T(8,128)S(1)} %get-tuple-element.31) | copy-start | bytes 589828
  72.8 2.6 %collective-permute-start.12 = (f32[2,1,192,128]{3,2,0,1:T(8,128)S(1)}, f32[2,1,192,128]{3,2,0,1:T(8,128)S(1)}, u32[]{:S(2)}, u32[]{:S(2)}) collective-permute-start(f32[2,1,192,128]{3,2,0,1:T(8,128)S(1)} %get-tuple-element.60), channel_id=1, source_target_pairs={{0,16},{1,17},{2,18},{3,19},{4,20},{5,21},{6,22},{7,23},{8,24},{9,... | collective-permute-start | bytes 589832 | tf_op jit(solution)/shard_map/ppermute | solution.py:24
  74.1 3.3 %collective-permute-start.13 = (f32[2,1,192,128]{3,2,0,1:T(8,128)S(1)}, f32[2,1,192,128]{3,2,0,1:T(8,128)S(1)}, u32[]{:S(2)}, u32[]{:S(2)}) collective-permute-start(f32[2,1,192,128]{3,2,0,1:T(8,128)S(1)} %get-tuple-element.61), channel_id=1, source_target_pairs={{16,0},{17,1},{18,2},{19,3},{20,4},{21,5},{22,6},{23,7},{24,8},{25... | collective-permute-start | bytes 589832 | tf_op jit(solution)/shard_map/ppermute | solution.py:25
  78.8 6.5 %collective-permute-start.14 = (f32[2,4,192,1]{2,1,3,0:T(4,128)S(1)}, f32[2,4,192,1]{2,1,3,0:T(4,128)S(1)}, u32[]{:S(2)}, u32[]{:S(2)}) collective-permute-start(f32[2,4,192,1]{2,1,3,0:T(4,128)S(1)} %copy.24), channel_id=1, source_target_pairs={{0,2},{2,4},{4,6},{6,8},{8,10},{10,12},{12,14},{1,3},{3,5},{5,7},{... | collective-permute-start | bytes 18440 | tf_op jit(solution)/shard_map/ppermute | solution.py:24
  84.0 6.7 %collective-permute-start.15 = (f32[2,4,192,1]{2,1,3,0:T(4,128)S(1)}, f32[2,4,192,1]{2,1,3,0:T(4,128)S(1)}, u32[]{:S(2)}, u32[]{:S(2)}) collective-permute-start(f32[2,4,192,1]{2,1,3,0:T(4,128)S(1)} %copy.25), channel_id=1, source_target_pairs={{2,0},{4,2},{6,4},{8,6},{10,8},{12,10},{14,12},{3,1},{5,3},{7,5},{... | collective-permute-start | bytes 18440 | tf_op jit(solution)/shard_map/ppermute | solution.py:25
  91.9 9.4 %collective-permute-start.16 = (f32[2,4,1,130]{3,2,0,1:T(1,128)S(1)}, f32[2,4,1,130]{3,2,0,1:T(1,128)S(1)}, u32[]{:S(2)}, u32[]{:S(2)}) collective-permute-start(f32[2,4,1,130]{3,2,0,1:T(1,128)S(1)} %get-tuple-element.40), channel_id=1, source_target_pairs={{0,1},{2,3},{4,5},{6,7},{8,9},{10,11},{12,13},{14,15},{16,17},{18,... | collective-permute-start | bytes 12488 | tf_op jit(solution)/shard_map/ppermute | solution.py:24
  93.5 7.7 %collective-permute-start.17 = (f32[2,4,1,130]{3,2,0,1:T(1,128)S(1)}, f32[2,4,1,130]{3,2,0,1:T(1,128)S(1)}, u32[]{:S(2)}, u32[]{:S(2)}) collective-permute-start(f32[2,4,1,130]{3,2,0,1:T(1,128)S(1)} %get-tuple-element.41), channel_id=1, source_target_pairs={{1,0},{3,2},{5,4},{7,6},{9,8},{11,10},{13,12},{15,14},{17,16},{19,... | collective-permute-start | bytes 12488 | tf_op jit(solution)/shard_map/ppermute | solution.py:25
  134.0 11.0 %collective-permute-start.18 = (f32[2,1,192,128]{3,2,0,1:T(8,128)S(1)}, f32[2,1,192,128]{3,2,0,1:T(8,128)S(1)}, u32[]{:S(2)}, u32[]{:S(2)}) collective-permute-start(f32[2,1,192,128]{3,2,0,1:T(8,128)S(1)} %get-tuple-element.56), channel_id=1, source_target_pairs={{0,16},{1,17},{2,18},{3,19},{4,20},{5,21},{6,22},{7,23},{8,24},{9,... | collective-permute-start | bytes 589832 | tf_op jit(solution)/shard_map/ppermute | solution.py:24
  135.3 9.7 %collective-permute-start.19 = (f32[2,1,192,128]{3,2,0,1:T(8,128)S(1)}, f32[2,1,192,128]{3,2,0,1:T(8,128)S(1)}, u32[]{:S(2)}, u32[]{:S(2)}) collective-permute-start(f32[2,1,192,128]{3,2,0,1:T(8,128)S(1)} %get-tuple-element.57), channel_id=1, source_target_pairs={{16,0},{17,1},{18,2},{19,3},{20,4},{21,5},{22,6},{23,7},{24,8},{25... | collective-permute-start | bytes 589832 | tf_op jit(solution)/shard_map/ppermute | solution.py:25
  146.4 8.1 %collective-permute-start.21 = (f32[2,4,192,1]{2,1,3,0:T(4,128)S(1)}, f32[2,4,192,1]{2,1,3,0:T(4,128)S(1)}, u32[]{:S(2)}, u32[]{:S(2)}) collective-permute-start(f32[2,4,192,1]{2,1,3,0:T(4,128)S(1)} %copy.32), channel_id=1, source_target_pairs={{2,0},{4,2},{6,4},{8,6},{10,8},{12,10},{14,12},{3,1},{5,3},{7,5},{... | collective-permute-start | bytes 18440 | tf_op jit(solution)/shard_map/ppermute | solution.py:25
  147.7 6.4 %collective-permute-start.20 = (f32[2,4,192,1]{2,1,3,0:T(4,128)S(1)}, f32[2,4,192,1]{2,1,3,0:T(4,128)S(1)}, u32[]{:S(2)}, u32[]{:S(2)}) collective-permute-start(f32[2,4,192,1]{2,1,3,0:T(4,128)S(1)} %copy.31), channel_id=1, source_target_pairs={{0,2},{2,4},{4,6},{6,8},{8,10},{10,12},{12,14},{1,3},{3,5},{5,7},{... | collective-permute-start | bytes 18440 | tf_op jit(solution)/shard_map/ppermute | solution.py:24
  155.7 5.3 %collective-permute-start.22 = (f32[2,4,1,130]{3,2,0,1:T(1,128)S(1)}, f32[2,4,1,130]{3,2,0,1:T(1,128)S(1)}, u32[]{:S(2)}, u32[]{:S(2)}) collective-permute-start(f32[2,4,1,130]{3,2,0,1:T(1,128)S(1)} %get-tuple-element.38), channel_id=1, source_target_pairs={{0,1},{2,3},{4,5},{6,7},{8,9},{10,11},{12,13},{14,15},{16,17},{18,... | collective-permute-start | bytes 12488 | tf_op jit(solution)/shard_map/ppermute | solution.py:24
  159.7 5.5 %collective-permute-start.23 = (f32[2,4,1,130]{3,2,0,1:T(1,128)S(1)}, f32[2,4,1,130]{3,2,0,1:T(1,128)S(1)}, u32[]{:S(2)}, u32[]{:S(2)}) collective-permute-start(f32[2,4,1,130]{3,2,0,1:T(1,128)S(1)} %get-tuple-element.39), channel_id=1, source_target_pairs={{1,0},{3,2},{5,4},{7,6},{9,8},{11,10},{13,12},{15,14},{17,16},{19,... | collective-permute-start | bytes 12488 | tf_op jit(solution)/shard_map/ppermute | solution.py:25
  169.3 2.6 %collective-permute-start.24 = (f32[2,1,192,128]{3,2,0,1:T(8,128)S(1)}, f32[2,1,192,128]{3,2,0,1:T(8,128)S(1)}, u32[]{:S(2)}, u32[]{:S(2)}) collective-permute-start(f32[2,1,192,128]{3,2,0,1:T(8,128)S(1)} %get-tuple-element.54), channel_id=1, source_target_pairs={{0,16},{1,17},{2,18},{3,19},{4,20},{5,21},{6,22},{7,23},{8,24},{9,... | collective-permute-start | bytes 589832 | tf_op jit(solution)/shard_map/ppermute | solution.py:24
  170.6 3.3 %collective-permute-start.25 = (f32[2,1,192,128]{3,2,0,1:T(8,128)S(1)}, f32[2,1,192,128]{3,2,0,1:T(8,128)S(1)}, u32[]{:S(2)}, u32[]{:S(2)}) collective-permute-start(f32[2,1,192,128]{3,2,0,1:T(8,128)S(1)} %get-tuple-element.55), channel_id=1, source_target_pairs={{16,0},{17,1},{18,2},{19,3},{20,4},{21,5},{22,6},{23,7},{24,8},{25... | collective-permute-start | bytes 589832 | tf_op jit(solution)/shard_map/ppermute | solution.py:25
  175.3 6.4 %collective-permute-start.26 = (f32[2,4,192,1]{2,1,3,0:T(4,128)S(1)}, f32[2,4,192,1]{2,1,3,0:T(4,128)S(1)}, u32[]{:S(2)}, u32[]{:S(2)}) collective-permute-start(f32[2,4,192,1]{2,1,3,0:T(4,128)S(1)} %copy.35), channel_id=1, source_target_pairs={{0,2},{2,4},{4,6},{6,8},{8,10},{10,12},{12,14},{1,3},{3,5},{5,7},{... | collective-permute-start | bytes 18440 | tf_op jit(solution)/shard_map/ppermute | solution.py:24
  180.4 6.2 %collective-permute-start.27 = (f32[2,4,192,1]{2,1,3,0:T(4,128)S(1)}, f32[2,4,192,1]{2,1,3,0:T(4,128)S(1)}, u32[]{:S(2)}, u32[]{:S(2)}) collective-permute-start(f32[2,4,192,1]{2,1,3,0:T(4,128)S(1)} %copy.36), channel_id=1, source_target_pairs={{2,0},{4,2},{6,4},{8,6},{10,8},{12,10},{14,12},{3,1},{5,3},{7,5},{... | collective-permute-start | bytes 18440 | tf_op jit(solution)/shard_map/ppermute | solution.py:25
  187.7 3.0 %collective-permute-start.28 = (f32[2,4,1,130]{3,2,0,1:T(1,128)S(1)}, f32[2,4,1,130]{3,2,0,1:T(1,128)S(1)}, u32[]{:S(2)}, u32[]{:S(2)}) collective-permute-start(f32[2,4,1,130]{3,2,0,1:T(1,128)S(1)} %get-tuple-element.36), channel_id=1, source_target_pairs={{0,1},{2,3},{4,5},{6,7},{8,9},{10,11},{12,13},{14,15},{16,17},{18,... | collective-permute-start | bytes 12488 | tf_op jit(solution)/shard_map/ppermute | solution.py:24
  189.4 5.5 %collective-permute-start.29 = (f32[2,4,1,130]{3,2,0,1:T(1,128)S(1)}, f32[2,4,1,130]{3,2,0,1:T(1,128)S(1)}, u32[]{:S(2)}, u32[]{:S(2)}) collective-permute-start(f32[2,4,1,130]{3,2,0,1:T(1,128)S(1)} %get-tuple-element.37), channel_id=1, source_target_pairs={{1,0},{3,2},{5,4},{7,6},{9,8},{11,10},{13,12},{15,14},{17,16},{19,... | collective-permute-start | bytes 12488 | tf_op jit(solution)/shard_map/ppermute | solution.py:25
  (16 other events, 50.4 us)
where the time goes:
time: 237 us; the launch traced here: 236 us
  blocking collectives  69.3 us (29%)
  starting transfers between devices  67.3 us (28%)
  waiting for transfers between devices  43.7 us (18%)
  other arithmetic  24.9 us (11%)
  local copies, waits for them, and re-layouts  23.5 us (10%)
  matrix products  5.73 us (2%)
    all_gather x2, blocking collectives, fold_traces(): lax.all_gather(mine, 'wide', axis=2, tiled=True)  52 us
    ppermute x15, starting transfers between devices, with_halo(): before = lax.ppermute(last, axis, up)  47.9 us
    ppermute x15, waiting for transfers between devices, with_halo(): after = lax.ppermute(first, axis, down)  27 us
    ppermute x15, starting transfers between devices, with_halo(): after = lax.ppermute(first, axis, down)  19.4 us
    ppermute x15, waiting for transfers between devices, with_halo(): before = lax.ppermute(last, axis, up)  16.7 us
    mul x5, other arithmetic, apply_operator(): weighted = box_sum(padded * cond_pad) - conductance * center  11.6 us
    psum x2, blocking collectives, local(): summed = lax.psum(partial_rows, 'narrow')  10.5 us
    reshape x1, local copies, waits for them, and re-layouts, local(): plane = boundary_operator.reshape(tile_rows, BY, -1)  6.41 us
  transfers between devices with their start and end apart: 30, of which 11 were waited for; matrix products, arithmetic and copies ran while one was open for 6% of the time, Pallas kernels for 0%

commit v1 on v0

--- a/solution.py
+++ b/solution.py
@@ -12,6 +12,18 @@
 upper_edge = 1.75
 mass_ratio = 26.0
 couple_gain = 40.0
+
+
+def summed_around(x, axis, dim, product):
+    size, index = (lax.axis_size(axis), lax.axis_index(axis))
+    left = [(i, (i - 1) % size) for i in range(size)]
+    width = x.shape[dim]
+    block = x
+    total = product(block, index * width)
+    for step in range(1, size):
+        block = lax.ppermute(block, axis, left)
+        total = total + product(block, (index + step) % size * width)
+    return total
 
 
 def with_halo(shard, sides, width):
@@ -68,11 +80,16 @@
 
 
 def fold_traces(mine, plane):
-    return jnp.einsum(
-        "ryx,kyx->rk",
-        plane,
-        lax.all_gather(mine, "wide", axis=2, tiled=True),
-        preferred_element_type=jnp.float32,
+    return summed_around(
+        mine,
+        "wide",
+        2,
+        lambda part, offset: jnp.einsum(
+            "ryx,kyx->rk",
+            lax.dynamic_slice_in_dim(plane, offset, part.shape[2], axis=2),
+            part,
+            preferred_element_type=jnp.float32,
+        ),
     )
 
 

time: 237 us -> 265 us (1.12)
  starting transfers between devices: 67.3 us -> 150 us
  blocking collectives: 69.3 us -> 17.2 us
  waiting for transfers between devices: 43.7 us -> 33.7 us
  local copies, waits for them, and re-layouts: 23.5 us -> 27.7 us
    ppermute x0 -> x14, starting transfers between devices: none -> 65.9 us  [summed_around(): block = lax.ppermute(block, axis, left)]
    all_gather x2 -> x0, blocking collectives: 52 us -> none  [fold_traces(): lax.all_gather(mine, 'wide', axis=2, tiled=True)]
    ppermute x15, waiting for transfers between devices: 27 us -> 7.71 us  [with_halo(): after = lax.ppermute(first, axis, down)]
    ppermute x15, starting transfers between devices: 47.9 us -> 64.1 us  [with_halo(): before = lax.ppermute(last, axis, up)]
    ppermute x0 -> x14, waiting for transfers between devices: none -> 10.8 us  [summed_around(): block = lax.ppermute(block, axis, left)]
    reshape x1 -> x0, local copies, waits for them, and re-layouts: 6.41 us -> none  [local(): plane = boundary_operator.reshape(tile_rows, BY, -1)]
    unnamed x38 -> x61, local copies, waits for them, and re-layouts: 6.24 us -> 12.6 us
    dynamic_slice x0 -> x1, local copies, waits for them, and re-layouts: none -> 4.37 us  [fold_traces(): lax.dynamic_slice_in_dim(plane, offset, part.shape[2], axis=2)]
  transfers between devices with their start and end apart: 30 -> 44, of which waited for: 11 -> 21; matrix products, arithmetic and copies ran while one was open for 6% -> 10% of each run, Pallas kernels for 0% -> 0%
where the time goes in v1:
time: 265 us; the launch traced here: 264 us
  starting transfers between devices  150 us (57%)
  waiting for transfers between devices  33.7 us (13%)
  local copies, waits for them, and re-layouts  27.7 us (10%)
  other arithmetic  25.8 us (10%)
  blocking collectives  17.2 us (6%)
  matrix products  8.22 us (3%)
    ppermute x14, starting transfers between devices, summed_around(): block = lax.ppermute(block, axis, left)  65.9 us
    ppermute x15, starting transfers between devices, with_halo(): before = lax.ppermute(last, axis, up)  64.1 us
    ppermute x15, starting transfers between devices, with_halo(): after = lax.ppermute(first, axis, down)  19.5 us
    ppermute x15, waiting for transfers between devices, with_halo(): before = lax.ppermute(last, axis, up)  15.2 us
    unnamed x61, local copies, waits for them, and re-layouts  12.6 us
    mul x5, other arithmetic, apply_operator(): weighted = box_sum(padded * cond_pad) - conductance * center  11.5 us
    ppermute x14, waiting for transfers between devices, summed_around(): block = lax.ppermute(block, axis, left)  10.8 us
    psum x2, blocking collectives, local(): summed = lax.psum(partial_rows, 'narrow')  10.1 us
  transfers between devices with their start and end apart: 44, of which 21 were waited for; matrix products, arithmetic and copies ran while one was open for 10% of the time, Pallas kernels for 0%

profile of v1, /device:TPU:0, one launch (start us, length us, event | category | flops | bytes accessed | tf_op | source)
XLA Modules:
  0.0 263.7 jit_solution(11847850267165204872)
XLA Ops:
  2.2 6.7 %broadcast_multiply_fusion.5 = (f32[2,192,128]{2,1,0:T(8,128)}, f32[2,192,128]{2,1,0:T(8,128)S(1)}) fusion(f32[]{:T(128)} %bitcast.7, s32[2,192,128]{2,1,0:T(8,128)} %param.7, f32[]{:T(128)} %bitcast.6, f32[]{:T(128)} %bitcast.5, f32[]{:T(128)} %bitcast.4, f32[]{:T(128)} %bitcast.3, f32[]{:T(128)} %bitcast.2, f32[]{:T(128)} %bitcast.1, f32[]{:T(128)} %bitcast), kind=kLoop, calls=%fused_computation.157 | loop fusion | flops 1179648 | bytes 589856 | tf_op jit(solution)/shard_map/mul | solution.py:66
  15.8 5.5 %collective-permute-start.2 = (f32[4,192,1]{2,1,0:T(8,128)S(1)}, f32[4,192,1]{2,1,0:T(8,128)S(1)}, u32[]{:S(2)}, u32[]{:S(2)}) collective-permute-start(f32[4,192,1]{2,1,0:T(8,128)S(1)} %get-tuple-element.70), channel_id=1, source_target_pairs={{0,2},{2,4},{4,6},{6,8},{8,10},{10,12},{12,14},{1,3},{3,5},{5,7},{... | collective-permute-start | bytes 9224 | tf_op jit(solution)/shard_map/ppermute | solution.py:36
  21.3 7.7 %collective-permute-done.3 = f32[4,192,1]{2,1,0:T(8,128)S(1)} collective-permute-done((f32[4,192,1]{2,1,0:T(8,128)S(1)}, f32[4,192,1]{2,1,0:T(8,128)S(1)}, u32[]{:S(2)}, u32[]{:S(2)}) %collective-permute-start.3) | collective-permute-done | bytes 3104 | tf_op jit(solution)/shard_map/ppermute | solution.py:37
  29.0 8.6 %collective-permute-done.2 = f32[4,192,1]{2,1,0:T(8,128)S(1)} collective-permute-done((f32[4,192,1]{2,1,0:T(8,128)S(1)}, f32[4,192,1]{2,1,0:T(8,128)S(1)}, u32[]{:S(2)}, u32[]{:S(2)}) %collective-permute-start.2) | collective-permute-done | bytes 3104 | tf_op jit(solution)/shard_map/ppermute | solution.py:36
  39.0 4.5 %collective-permute-start.4 = (f32[4,1,130]{2,1,0:T(1,128)S(1)}, f32[4,1,130]{2,1,0:T(1,128)S(1)}, u32[]{:S(2)}, u32[]{:S(2)}) collective-permute-start(f32[4,1,130]{2,1,0:T(1,128)S(1)} %get-tuple-element.52), channel_id=1, source_target_pairs={{0,1},{2,3},{4,5},{6,7},{8,9},{10,11},{12,13},{14,15},{16,17},{18,... | collective-permute-start | bytes 6248 | tf_op jit(solution)/shard_map/ppermute | solution.py:36
  53.3 5.0 %collective-permute-start.8 = (f32[2,4,192,1]{2,1,3,0:T(4,128)S(1)}, f32[2,4,192,1]{2,1,3,0:T(4,128)S(1)}, u32[]{:S(2)}, u32[]{:S(2)}) collective-permute-start(f32[2,4,192,1]{2,1,3,0:T(4,128)S(1)} %copy.19), channel_id=1, source_target_pairs={{0,2},{2,4},{4,6},{6,8},{8,10},{10,12},{12,14},{1,3},{3,5},{5,7},{... | collective-permute-start | bytes 18440 | tf_op jit(solution)/shard_map/ppermute | solution.py:36
  61.4 4.5 %collective-permute-start.10 = (f32[2,4,1,130]{3,2,0,1:T(1,128)S(1)}, f32[2,4,1,130]{3,2,0,1:T(1,128)S(1)}, u32[]{:S(2)}, u32[]{:S(2)}) collective-permute-start(f32[2,4,1,130]{3,2,0,1:T(1,128)S(1)} %get-tuple-element.50), channel_id=1, source_target_pairs={{0,1},{2,3},{4,5},{6,7},{8,9},{10,11},{12,13},{14,15},{16,17},{18,... | collective-permute-start | bytes 12488 | tf_op jit(solution)/shard_map/ppermute | solution.py:36
  73.3 3.7 %collective-permute-start.12 = (f32[2,1,192,128]{3,2,0,1:T(8,128)S(1)}, f32[2,1,192,128]{3,2,0,1:T(8,128)}, u32[]{:S(2)}, u32[]{:S(2)}) collective-permute-start(f32[2,1,192,128]{3,2,0,1:T(8,128)S(1)} %get-tuple-element.68), channel_id=1, source_target_pairs={{0,16},{1,17},{2,18},{3,19},{4,20},{5,21},{6,22},{7,23},{8,24},{9,... | collective-permute-start | bytes 589832 | tf_op jit(solution)/shard_map/ppermute | solution.py:36
  80.7 5.4 %collective-permute-start.14 = (f32[2,4,192,1]{2,1,3,0:T(4,128)S(1)}, f32[2,4,192,1]{2,1,3,0:T(4,128)S(1)}, u32[]{:S(2)}, u32[]{:S(2)}) collective-permute-start(f32[2,4,192,1]{2,1,3,0:T(4,128)S(1)} %copy.24), channel_id=1, source_target_pairs={{0,2},{2,4},{4,6},{6,8},{8,10},{10,12},{12,14},{1,3},{3,5},{5,7},{... | collective-permute-start | bytes 18440 | tf_op jit(solution)/shard_map/ppermute | solution.py:36
  86.3 7.0 %copy.64 = bf16[16,8,16,1024]{3,2,1,0:T(8,128)(2,1)} copy(bf16[16,8,16,1024]{3,1,2,0:T(8,128)(2,1)} %bitcast.121) | data formatting | bytes 8388608
  96.0 4.7 %collective-permute-start.16 = (f32[2,4,1,130]{3,2,0,1:T(1,128)S(1)}, f32[2,4,1,130]{3,2,0,1:T(1,128)S(1)}, u32[]{:S(2)}, u32[]{:S(2)}) collective-permute-start(f32[2,4,1,130]{3,2,0,1:T(1,128)S(1)} %get-tuple-element.48), channel_id=1, source_target_pairs={{0,1},{2,3},{4,5},{6,7},{8,9},{10,11},{12,13},{14,15},{16,17},{18,... | collective-permute-start | bytes 12488 | tf_op jit(solution)/shard_map/ppermute | solution.py:36
  100.8 4.4 %constant_dynamic-slice_fusion.3 = (bf16[128,16,128]{2,1,0:T(8,128)(2,1)}, bf16[128,16,128]{2,1,0:T(8,128)(2,1)}, bf16[128,16,128]{2,1,0:T(8,128)(2,1)}, bf16[12...) fusion(bf16[128,16,1024]{2,1,0:T(8,128)(2,1)} %bitcast.120, ...), kind=kLoop, calls=%fused_computation.204 | loop fusion | bytes 8388640 | tf_op jit(solution)/shard_map/dynamic_slice | solution.py:89
  112.0 4.6 %collective-permute-start.18 = (bf16[1,16,128]{2,1,0:T(8,128)(2,1)S(1)}, bf16[1,16,128]{2,1,0:T(8,128)(2,1)S(1)}, u32[]{:S(2)}, u32[]{:S(2)}) collective-permute-start(bf16[1,16,128]{2,1,0:T(8,128)(2,1)S(1)} %constant_dynamic-slice_fusion.10), channel_id=1, source_target_pairs={{0,14},{2,0},{4,2},{6,4},{8,6},{10,8},{12,10},{14,12},{1,15},{3,1}... | collective-permute-start | bytes 12296 | tf_op jit(solution)/shard_map/ppermute | solution.py:24
  118.1 3.0 %collective-permute-start.25 = (f32[2,1,192,128]{3,2,0,1:T(8,128)S(1)}, f32[2,1,192,128]{3,2,0,1:T(8,128)S(1)}, u32[]{:S(2)}, u32[]{:S(2)}) collective-permute-start(f32[2,1,192,128]{3,2,0,1:T(8,128)S(1)} %get-tuple-element.64), channel_id=1, source_target_pairs={{0,16},{1,17},{2,18},{3,19},{4,20},{5,21},{6,22},{7,23},{8,24},{9,... | collective-permute-start | bytes 589832 | tf_op jit(solution)/shard_map/ppermute | solution.py:36
  126.5 5.0 %collective-permute-start.20 = (bf16[1,16,128]{2,1,0:T(8,128)(2,1)S(1)}, bf16[1,16,128]{2,1,0:T(8,128)(2,1)S(1)}, u32[]{:S(2)}, u32[]{:S(2)}) collective-permute-start(bf16[1,16,128]{2,1,0:T(8,128)(2,1)S(1)} %collective-permute-done.19), channel_id=1, source_target_pairs={{0,14},{2,0},{4,2},{6,4},{8,6},{10,8},{12,10},{14,12},{1,15},{3,1}... | collective-permute-start | bytes 12296 | tf_op jit(solution)/shard_map/ppermute | solution.py:24
  132.8 5.0 %collective-permute-start.21 = (bf16[1,16,128]{2,1,0:T(8,128)(2,1)S(1)}, bf16[1,16,128]{2,1,0:T(8,128)(2,1)S(1)}, u32[]{:S(2)}, u32[]{:S(2)}) collective-permute-start(bf16[1,16,128]{2,1,0:T(8,128)(2,1)S(1)} %collective-permute-done.20), channel_id=1, source_target_pairs={{0,14},{2,0},{4,2},{6,4},{8,6},{10,8},{12,10},{14,12},{1,15},{3,1}... | collective-permute-start | bytes 12296 | tf_op jit(solution)/shard_map/ppermute | solution.py:24
  139.1 5.0 %collective-permute-start.22 = (bf16[1,16,128]{2,1,0:T(8,128)(2,1)S(1)}, bf16[1,16,128]{2,1,0:T(8,128)(2,1)S(1)}, u32[]{:S(2)}, u32[]{:S(2)}) collective-permute-start(bf16[1,16,128]{2,1,0:T(8,128)(2,1)S(1)} %collective-permute-done.21), channel_id=1, source_target_pairs={{0,14},{2,0},{4,2},{6,4},{8,6},{10,8},{12,10},{14,12},{1,15},{3,1}... | collective-permute-start | bytes 12296 | tf_op jit(solution)/shard_map/ppermute | solution.py:24
  145.4 5.0 %collective-permute-start.23 = (bf16[1,16,128]{2,1,0:T(8,128)(2,1)S(1)}, bf16[1,16,128]{2,1,0:T(8,128)(2,1)S(1)}, u32[]{:S(2)}, u32[]{:S(2)}) collective-permute-start(bf16[1,16,128]{2,1,0:T(8,128)(2,1)S(1)} %collective-permute-done.22), channel_id=1, source_target_pairs={{0,14},{2,0},{4,2},{6,4},{8,6},{10,8},{12,10},{14,12},{1,15},{3,1}... | collective-permute-start | bytes 12296 | tf_op jit(solution)/shard_map/ppermute | solution.py:24
  151.7 5.0 %collective-permute-start.24 = (bf16[1,16,128]{2,1,0:T(8,128)(2,1)S(1)}, bf16[1,16,128]{2,1,0:T(8,128)(2,1)S(1)}, u32[]{:S(2)}, u32[]{:S(2)}) collective-permute-start(bf16[1,16,128]{2,1,0:T(8,128)(2,1)S(1)} %collective-permute-done.23), channel_id=1, source_target_pairs={{0,14},{2,0},{4,2},{6,4},{8,6},{10,8},{12,10},{14,12},{1,15},{3,1}... | collective-permute-start | bytes 12296 | tf_op jit(solution)/shard_map/ppermute | solution.py:24
  158.2 4.9 %psum.29 = f32[128,1]{0,1:T(1,128)S(1)} all-reduce(f32[128,1]{0,1:T(1,128)S(1)} %fusion.9), channel_id=1, replica_groups=mesh['vol'=2,'wide'=8,'narrow'=2] {'narrow'}, use_global_device_ids=true, to_apply=%region_1.2 | all-reduce | flops 128 | bytes 1024 | tf_op jit(solution)/shard_map/psum | solution.py:124
  165.9 4.5 %collective-permute-start.27 = (f32[2,4,192,1]{2,1,3,0:T(4,128)S(1)}, f32[2,4,192,1]{2,1,3,0:T(4,128)S(1)}, u32[]{:S(2)}, u32[]{:S(2)}) collective-permute-start(f32[2,4,192,1]{2,1,3,0:T(4,128)S(1)} %copy.31), channel_id=1, source_target_pairs={{0,2},{2,4},{4,6},{6,8},{8,10},{10,12},{12,14},{1,3},{3,5},{5,7},{... | collective-permute-start | bytes 18440 | tf_op jit(solution)/shard_map/ppermute | solution.py:36
  175.2 4.5 %collective-permute-start.29 = (f32[2,4,1,130]{3,2,0,1:T(1,128)S(1)}, f32[2,4,1,130]{3,2,0,1:T(1,128)S(1)}, u32[]{:S(2)}, u32[]{:S(2)}) collective-permute-start(f32[2,4,1,130]{3,2,0,1:T(1,128)S(1)} %get-tuple-element.46), channel_id=1, source_target_pairs={{0,1},{2,3},{4,5},{6,7},{8,9},{10,11},{12,13},{14,15},{16,17},{18,... | collective-permute-start | bytes 12488 | tf_op jit(solution)/shard_map/ppermute | solution.py:36
  193.5 4.5 %collective-permute-start.33 = (f32[2,4,192,1]{2,1,3,0:T(4,128)S(1)}, f32[2,4,192,1]{2,1,3,0:T(4,128)S(1)}, u32[]{:S(2)}, u32[]{:S(2)}) collective-permute-start(f32[2,4,192,1]{2,1,3,0:T(4,128)S(1)} %copy.35), channel_id=1, source_target_pairs={{0,2},{2,4},{4,6},{6,8},{8,10},{10,12},{12,14},{1,3},{3,5},{5,7},{... | collective-permute-start | bytes 18440 | tf_op jit(solution)/shard_map/ppermute | solution.py:36
  201.9 4.8 %collective-permute-start.35 = (f32[2,4,1,130]{3,2,0,1:T(1,128)S(1)}, f32[2,4,1,130]{3,2,0,1:T(1,128)S(1)}, u32[]{:S(2)}, u32[]{:S(2)}) collective-permute-start(f32[2,4,1,130]{3,2,0,1:T(1,128)S(1)} %get-tuple-element.44), channel_id=1, source_target_pairs={{0,1},{2,3},{4,5},{6,7},{8,9},{10,11},{12,13},{14,15},{16,17},{18,... | collective-permute-start | bytes 12488 | tf_op jit(solution)/shard_map/ppermute | solution.py:36
  213.9 4.7 %collective-permute-start.37 = (bf16[1,16,128]{2,1,0:T(8,128)(2,1)S(1)}, bf16[1,16,128]{2,1,0:T(8,128)(2,1)S(1)}, u32[]{:S(2)}, u32[]{:S(2)}) collective-permute-start(bf16[1,16,128]{2,1,0:T(8,128)(2,1)S(1)} %constant_dynamic-slice_fusion.1), channel_id=1, source_target_pairs={{0,14},{2,0},{4,2},{6,4},{8,6},{10,8},{12,10},{14,12},{1,15},{3,1}... | collective-permute-start | bytes 12296 | tf_op jit(solution)/shard_map/ppermute | solution.py:24
  220.6 4.2 %collective-permute-start.38 = (bf16[1,16,128]{2,1,0:T(8,128)(2,1)S(1)}, bf16[1,16,128]{2,1,0:T(8,128)(2,1)S(1)}, u32[]{:S(2)}, u32[]{:S(2)}) collective-permute-start(bf16[1,16,128]{2,1,0:T(8,128)(2,1)S(1)} %collective-permute-done.37), channel_id=1, source_target_pairs={{0,14},{2,0},{4,2},{6,4},{8,6},{10,8},{12,10},{14,12},{1,15},{3,1}... | collective-permute-start | bytes 12296 | tf_op jit(solution)/shard_map/ppermute | solution.py:24
  226.2 5.0 %collective-permute-start.39 = (bf16[1,16,128]{2,1,0:T(8,128)(2,1)S(1)}, bf16[1,16,128]{2,1,0:T(8,128)(2,1)S(1)}, u32[]{:S(2)}, u32[]{:S(2)}) collective-permute-start(bf16[1,16,128]{2,1,0:T(8,128)(2,1)S(1)} %collective-permute-done.38), channel_id=1, source_target_pairs={{0,14},{2,0},{4,2},{6,4},{8,6},{10,8},{12,10},{14,12},{1,15},{3,1}... | collective-permute-start | bytes 12296 | tf_op jit(solution)/shard_map/ppermute | solution.py:24
  232.5 5.0 %collective-permute-start.40 = (bf16[1,16,128]{2,1,0:T(8,128)(2,1)S(1)}, bf16[1,16,128]{2,1,0:T(8,128)(2,1)S(1)}, u32[]{:S(2)}, u32[]{:S(2)}) collective-permute-start(bf16[1,16,128]{2,1,0:T(8,128)(2,1)S(1)} %collective-permute-done.39), channel_id=1, source_target_pairs={{0,14},{2,0},{4,2},{6,4},{8,6},{10,8},{12,10},{14,12},{1,15},{3,1}... | collective-permute-start | bytes 12296 | tf_op jit(solution)/shard_map/ppermute | solution.py:24
  238.8 5.0 %collective-permute-start.41 = (bf16[1,16,128]{2,1,0:T(8,128)(2,1)S(1)}, bf16[1,16,128]{2,1,0:T(8,128)(2,1)S(1)}, u32[]{:S(2)}, u32[]{:S(2)}) collective-permute-start(bf16[1,16,128]{2,1,0:T(8,128)(2,1)S(1)} %collective-permute-done.40), channel_id=1, source_target_pairs={{0,14},{2,0},{4,2},{6,4},{8,6},{10,8},{12,10},{14,12},{1,15},{3,1}... | collective-permute-start | bytes 12296 | tf_op jit(solution)/shard_map/ppermute | solution.py:24
  245.1 5.0 %collective-permute-start.42 = (bf16[1,16,128]{2,1,0:T(8,128)(2,1)S(1)}, bf16[1,16,128]{2,1,0:T(8,128)(2,1)S(1)}, u32[]{:S(2)}, u32[]{:S(2)}) collective-permute-start(bf16[1,16,128]{2,1,0:T(8,128)(2,1)S(1)} %collective-permute-done.41), channel_id=1, source_target_pairs={{0,14},{2,0},{4,2},{6,4},{8,6},{10,8},{12,10},{14,12},{1,15},{3,1}... | collective-permute-start | bytes 12296 | tf_op jit(solution)/shard_map/ppermute | solution.py:24
  251.4 5.0 %collective-permute-start.43 = (bf16[1,16,128]{2,1,0:T(8,128)(2,1)S(1)}, bf16[1,16,128]{2,1,0:T(8,128)(2,1)S(1)}, u32[]{:S(2)}, u32[]{:S(2)}) collective-permute-start(bf16[1,16,128]{2,1,0:T(8,128)(2,1)S(1)} %collective-permute-done.42), channel_id=1, source_target_pairs={{0,14},{2,0},{4,2},{6,4},{8,6},{10,8},{12,10},{14,12},{1,15},{3,1}... | collective-permute-start | bytes 12296 | tf_op jit(solution)/shard_map/ppermute | solution.py:24
  257.9 5.2 %psum.31 = f32[128,1]{0,1:T(1,128)S(1)} all-reduce(f32[128,1]{0,1:T(1,128)S(1)} %fusion.1), channel_id=1, replica_groups=mesh['vol'=2,'wide'=8,'narrow'=2] {'narrow'}, use_global_device_ids=true, to_apply=%region_3.4 | all-reduce | flops 128 | bytes 1024 | tf_op jit(solution)/shard_map/psum | solution.py:124
  (215 shorter events, 99.4 us)
Async XLA Ops:
  14.5 14.5 %collective-permute-start.3 = (f32[4,192,1]{2,1,0:T(8,128)S(1)}, f32[4,192,1]{2,1,0:T(8,128)S(1)}, u32[]{:S(2)}, u32[]{:S(2)}) collective-permute-start(f32[4,192,1]{2,1,0:T(8,128)S(1)} %get-tuple-element.71), channel_id=1, source_target_pairs={{2,0},{4,2},{6,4},{8,6},{10,8},{12,10},{14,12},{3,1},{5,3},{7,5},{... | collective-permute-start | bytes 9224 | tf_op jit(solution)/shard_map/ppermute | solution.py:37
  15.8 21.8 %collective-permute-start.2 = (f32[4,192,1]{2,1,0:T(8,128)S(1)}, f32[4,192,1]{2,1,0:T(8,128)S(1)}, u32[]{:S(2)}, u32[]{:S(2)}) collective-permute-start(f32[4,192,1]{2,1,0:T(8,128)S(1)} %get-tuple-element.70), channel_id=1, source_target_pairs={{0,2},{2,4},{4,6},{6,8},{8,10},{10,12},{12,14},{1,3},{3,5},{5,7},{... | collective-permute-start | bytes 9224 | tf_op jit(solution)/shard_map/ppermute | solution.py:36
  37.7 10.2 %collective-permute-start.5 = (f32[4,1,130]{2,1,0:T(1,128)S(1)}, f32[4,1,130]{2,1,0:T(1,128)S(1)}, u32[]{:S(2)}, u32[]{:S(2)}) collective-permute-start(f32[4,1,130]{2,1,0:T(1,128)S(1)} %get-tuple-element.53), channel_id=1, source_target_pairs={{1,0},{3,2},{5,4},{7,6},{9,8},{11,10},{13,12},{15,14},{17,16},{19,... | collective-permute-start | bytes 6248 | tf_op jit(solution)/shard_map/ppermute | solution.py:37
  39.0 8.9 %collective-permute-start.4 = (f32[4,1,130]{2,1,0:T(1,128)S(1)}, f32[4,1,130]{2,1,0:T(1,128)S(1)}, u32[]{:S(2)}, u32[]{:S(2)}) collective-permute-start(f32[4,1,130]{2,1,0:T(1,128)S(1)} %get-tuple-element.52), channel_id=1, source_target_pairs={{0,1},{2,3},{4,5},{6,7},{8,9},{10,11},{12,13},{14,15},{16,17},{18,... | collective-permute-start | bytes 6248 | tf_op jit(solution)/shard_map/ppermute | solution.py:36
  51.6 7.5 %collective-permute-start.9 = (f32[2,4,192,1]{2,1,3,0:T(4,128)S(1)}, f32[2,4,192,1]{2,1,3,0:T(4,128)S(1)}, u32[]{:S(2)}, u32[]{:S(2)}) collective-permute-start(f32[2,4,192,1]{2,1,3,0:T(4,128)S(1)} %copy.20), channel_id=1, source_target_pairs={{2,0},{4,2},{6,4},{8,6},{10,8},{12,10},{14,12},{3,1},{5,3},{7,5},{... | collective-permute-start | bytes 18440 | tf_op jit(solution)/shard_map/ppermute | solution.py:37
  53.3 6.3 %collective-permute-start.8 = (f32[2,4,192,1]{2,1,3,0:T(4,128)S(1)}, f32[2,4,192,1]{2,1,3,0:T(4,128)S(1)}, u32[]{:S(2)}, u32[]{:S(2)}) collective-permute-start(f32[2,4,192,1]{2,1,3,0:T(4,128)S(1)} %copy.19), channel_id=1, source_target_pairs={{0,2},{2,4},{4,6},{6,8},{8,10},{10,12},{12,14},{1,3},{3,5},{5,7},{... | collective-permute-start | bytes 18440 | tf_op jit(solution)/shard_map/ppermute | solution.py:36
  60.1 7.0 %collective-permute-start.11 = (f32[2,4,1,130]{3,2,0,1:T(1,128)S(1)}, f32[2,4,1,130]{3,2,0,1:T(1,128)S(1)}, u32[]{:S(2)}, u32[]{:S(2)}) collective-permute-start(f32[2,4,1,130]{3,2,0,1:T(1,128)S(1)} %get-tuple-element.51), channel_id=1, source_target_pairs={{1,0},{3,2},{5,4},{7,6},{9,8},{11,10},{13,12},{15,14},{17,16},{19,... | collective-permute-start | bytes 12488 | tf_op jit(solution)/shard_map/ppermute | solution.py:37
  79.1 14.2 %collective-permute-start.15 = (f32[2,4,192,1]{2,1,3,0:T(4,128)S(1)}, f32[2,4,192,1]{2,1,3,0:T(4,128)S(1)}, u32[]{:S(2)}, u32[]{:S(2)}) collective-permute-start(f32[2,4,192,1]{2,1,3,0:T(4,128)S(1)} %copy.25), channel_id=1, source_target_pairs={{2,0},{4,2},{6,4},{8,6},{10,8},{12,10},{14,12},{3,1},{5,3},{7,5},{... | collective-permute-start | bytes 18440 | tf_op jit(solution)/shard_map/ppermute | solution.py:37
  80.7 12.8 %collective-permute-start.14 = (f32[2,4,192,1]{2,1,3,0:T(4,128)S(1)}, f32[2,4,192,1]{2,1,3,0:T(4,128)S(1)}, u32[]{:S(2)}, u32[]{:S(2)}) collective-permute-start(f32[2,4,192,1]{2,1,3,0:T(4,128)S(1)} %copy.24), channel_id=1, source_target_pairs={{0,2},{2,4},{4,6},{6,8},{8,10},{10,12},{12,14},{1,3},{3,5},{5,7},{... | collective-permute-start | bytes 18440 | tf_op jit(solution)/shard_map/ppermute | solution.py:36
  94.7 10.4 %collective-permute-start.17 = (f32[2,4,1,130]{3,2,0,1:T(1,128)S(1)}, f32[2,4,1,130]{3,2,0,1:T(1,128)S(1)}, u32[]{:S(2)}, u32[]{:S(2)}) collective-permute-start(f32[2,4,1,130]{3,2,0,1:T(1,128)S(1)} %get-tuple-element.49), channel_id=1, source_target_pairs={{1,0},{3,2},{5,4},{7,6},{9,8},{11,10},{13,12},{15,14},{17,16},{19,... | collective-permute-start | bytes 12488 | tf_op jit(solution)/shard_map/ppermute | solution.py:37
  96.0 9.1 %collective-permute-start.16 = (f32[2,4,1,130]{3,2,0,1:T(1,128)S(1)}, f32[2,4,1,130]{3,2,0,1:T(1,128)S(1)}, u32[]{:S(2)}, u32[]{:S(2)}) collective-permute-start(f32[2,4,1,130]{3,2,0,1:T(1,128)S(1)} %get-tuple-element.48), channel_id=1, source_target_pairs={{0,1},{2,3},{4,5},{6,7},{8,9},{10,11},{12,13},{14,15},{16,17},{18,... | collective-permute-start | bytes 12488 | tf_op jit(solution)/shard_map/ppermute | solution.py:36
  112.0 10.5 %collective-permute-start.18 = (bf16[1,16,128]{2,1,0:T(8,128)(2,1)S(1)}, bf16[1,16,128]{2,1,0:T(8,128)(2,1)S(1)}, u32[]{:S(2)}, u32[]{:S(2)}) collective-permute-start(bf16[1,16,128]{2,1,0:T(8,128)(2,1)S(1)} %constant_dynamic-slice_fusion.10), channel_id=1, source_target_pairs={{0,14},{2,0},{4,2},{6,4},{8,6},{10,8},{12,10},{14,12},{1,15},{3,1}... | collective-permute-start | bytes 12296 | tf_op jit(solution)/shard_map/ppermute | solution.py:24
  116.6 46.5 %collective-permute-start.26 = (f32[2,1,192,128]{3,2,0,1:T(8,128)S(1)}, f32[2,1,192,128]{3,2,0,1:T(8,128)S(1)}, u32[]{:S(2)}, u32[]{:S(2)}) collective-permute-start(f32[2,1,192,128]{3,2,0,1:T(8,128)S(1)} %get-tuple-element.65), channel_id=1, source_target_pairs={{16,0},{17,1},{18,2},{19,3},{20,4},{21,5},{22,6},{23,7},{24,8},{25... | collective-permute-start | bytes 589832 | tf_op jit(solution)/shard_map/ppermute | solution.py:37
  118.1 45.1 %collective-permute-start.25 = (f32[2,1,192,128]{3,2,0,1:T(8,128)S(1)}, f32[2,1,192,128]{3,2,0,1:T(8,128)S(1)}, u32[]{:S(2)}, u32[]{:S(2)}) collective-permute-start(f32[2,1,192,128]{3,2,0,1:T(8,128)S(1)} %get-tuple-element.64), channel_id=1, source_target_pairs={{0,16},{1,17},{2,18},{3,19},{4,20},{5,21},{6,22},{7,23},{8,24},{9,... | collective-permute-start | bytes 589832 | tf_op jit(solution)/shard_map/ppermute | solution.py:36
  126.5 6.3 %collective-permute-start.20 = (bf16[1,16,128]{2,1,0:T(8,128)(2,1)S(1)}, bf16[1,16,128]{2,1,0:T(8,128)(2,1)S(1)}, u32[]{:S(2)}, u32[]{:S(2)}) collective-permute-start(bf16[1,16,128]{2,1,0:T(8,128)(2,1)S(1)} %collective-permute-done.19), channel_id=1, source_target_pairs={{0,14},{2,0},{4,2},{6,4},{8,6},{10,8},{12,10},{14,12},{1,15},{3,1}... | collective-permute-start | bytes 12296 | tf_op jit(solution)/shard_map/ppermute | solution.py:24
  132.8 6.3 %collective-permute-start.21 = (bf16[1,16,128]{2,1,0:T(8,128)(2,1)S(1)}, bf16[1,16,128]{2,1,0:T(8,128)(2,1)S(1)}, u32[]{:S(2)}, u32[]{:S(2)}) collective-permute-start(bf16[1,16,128]{2,1,0:T(8,128)(2,1)S(1)} %collective-permute-done.20), channel_id=1, source_target_pairs={{0,14},{2,0},{4,2},{6,4},{8,6},{10,8},{12,10},{14,12},{1,15},{3,1}... | collective-permute-start | bytes 12296 | tf_op jit(solution)/shard_map/ppermute | solution.py:24
  139.1 6.3 %collective-permute-start.22 = (bf16[1,16,128]{2,1,0:T(8,128)(2,1)S(1)}, bf16[1,16,128]{2,1,0:T(8,128)(2,1)S(1)}, u32[]{:S(2)}, u32[]{:S(2)}) collective-permute-start(bf16[1,16,128]{2,1,0:T(8,128)(2,1)S(1)} %collective-permute-done.21), channel_id=1, source_target_pairs={{0,14},{2,0},{4,2},{6,4},{8,6},{10,8},{12,10},{14,12},{1,15},{3,1}... | collective-permute-start | bytes 12296 | tf_op jit(solution)/shard_map/ppermute | solution.py:24
  145.4 6.3 %collective-permute-start.23 = (bf16[1,16,128]{2,1,0:T(8,128)(2,1)S(1)}, bf16[1,16,128]{2,1,0:T(8,128)(2,1)S(1)}, u32[]{:S(2)}, u32[]{:S(2)}) collective-permute-start(bf16[1,16,128]{2,1,0:T(8,128)(2,1)S(1)} %collective-permute-done.22), channel_id=1, source_target_pairs={{0,14},{2,0},{4,2},{6,4},{8,6},{10,8},{12,10},{14,12},{1,15},{3,1}... | collective-permute-start | bytes 12296 | tf_op jit(solution)/shard_map/ppermute | solution.py:24
  151.7 6.3 %collective-permute-start.24 = (bf16[1,16,128]{2,1,0:T(8,128)(2,1)S(1)}, bf16[1,16,128]{2,1,0:T(8,128)(2,1)S(1)}, u32[]{:S(2)}, u32[]{:S(2)}) collective-permute-start(bf16[1,16,128]{2,1,0:T(8,128)(2,1)S(1)} %collective-permute-done.23), channel_id=1, source_target_pairs={{0,14},{2,0},{4,2},{6,4},{8,6},{10,8},{12,10},{14,12},{1,15},{3,1}... | collective-permute-start | bytes 12296 | tf_op jit(solution)/shard_map/ppermute | solution.py:24
  164.3 8.1 %collective-permute-start.28 = (f32[2,4,192,1]{2,1,3,0:T(4,128)S(1)}, f32[2,4,192,1]{2,1,3,0:T(4,128)S(1)}, u32[]{:S(2)}, u32[]{:S(2)}) collective-permute-start(f32[2,4,192,1]{2,1,3,0:T(4,128)S(1)} %copy.32), channel_id=1, source_target_pairs={{2,0},{4,2},{6,4},{8,6},{10,8},{12,10},{14,12},{3,1},{5,3},{7,5},{... | collective-permute-start | bytes 18440 | tf_op jit(solution)/shard_map/ppermute | solution.py:37
  165.9 6.8 %collective-permute-start.27 = (f32[2,4,192,1]{2,1,3,0:T(4,128)S(1)}, f32[2,4,192,1]{2,1,3,0:T(4,128)S(1)}, u32[]{:S(2)}, u32[]{:S(2)}) collective-permute-start(f32[2,4,192,1]{2,1,3,0:T(4,128)S(1)} %copy.31), channel_id=1, source_target_pairs={{0,2},{2,4},{4,6},{6,8},{8,10},{10,12},{12,14},{1,3},{3,5},{5,7},{... | collective-permute-start | bytes 18440 | tf_op jit(solution)/shard_map/ppermute | solution.py:36
  173.9 5.9 %collective-permute-start.30 = (f32[2,4,1,130]{3,2,0,1:T(1,128)S(1)}, f32[2,4,1,130]{3,2,0,1:T(1,128)S(1)}, u32[]{:S(2)}, u32[]{:S(2)}) collective-permute-start(f32[2,4,1,130]{3,2,0,1:T(1,128)S(1)} %get-tuple-element.47), channel_id=1, source_target_pairs={{1,0},{3,2},{5,4},{7,6},{9,8},{11,10},{13,12},{15,14},{17,16},{19,... | collective-permute-start | bytes 12488 | tf_op jit(solution)/shard_map/ppermute | solution.py:37
  175.2 5.9 %collective-permute-start.29 = (f32[2,4,1,130]{3,2,0,1:T(1,128)S(1)}, f32[2,4,1,130]{3,2,0,1:T(1,128)S(1)}, u32[]{:S(2)}, u32[]{:S(2)}) collective-permute-start(f32[2,4,1,130]{3,2,0,1:T(1,128)S(1)} %get-tuple-element.46), channel_id=1, source_target_pairs={{0,1},{2,3},{4,5},{6,7},{8,9},{10,11},{12,13},{14,15},{16,17},{18,... | collective-permute-start | bytes 12488 | tf_op jit(solution)/shard_map/ppermute | solution.py:36
  191.9 6.2 %collective-permute-start.34 = (f32[2,4,192,1]{2,1,3,0:T(4,128)S(1)}, f32[2,4,192,1]{2,1,3,0:T(4,128)S(1)}, u32[]{:S(2)}, u32[]{:S(2)}) collective-permute-start(f32[2,4,192,1]{2,1,3,0:T(4,128)S(1)} %copy.36), channel_id=1, source_target_pairs={{2,0},{4,2},{6,4},{8,6},{10,8},{12,10},{14,12},{3,1},{5,3},{7,5},{... | collective-permute-start | bytes 18440 | tf_op jit(solution)/shard_map/ppermute | solution.py:37
  193.5 5.9 %collective-permute-start.33 = (f32[2,4,192,1]{2,1,3,0:T(4,128)S(1)}, f32[2,4,192,1]{2,1,3,0:T(4,128)S(1)}, u32[]{:S(2)}, u32[]{:S(2)}) collective-permute-start(f32[2,4,192,1]{2,1,3,0:T(4,128)S(1)} %copy.35), channel_id=1, source_target_pairs={{0,2},{2,4},{4,6},{6,8},{8,10},{10,12},{12,14},{1,3},{3,5},{5,7},{... | collective-permute-start | bytes 18440 | tf_op jit(solution)/shard_map/ppermute | solution.py:36
  200.6 6.1 %collective-permute-start.36 = (f32[2,4,1,130]{3,2,0,1:T(1,128)S(1)}, f32[2,4,1,130]{3,2,0,1:T(1,128)S(1)}, u32[]{:S(2)}, u32[]{:S(2)}) collective-permute-start(f32[2,4,1,130]{3,2,0,1:T(1,128)S(1)} %get-tuple-element.45), channel_id=1, source_target_pairs={{1,0},{3,2},{5,4},{7,6},{9,8},{11,10},{13,12},{15,14},{17,16},{19,... | collective-permute-start | bytes 12488 | tf_op jit(solution)/shard_map/ppermute | solution.py:37
  213.9 6.7 %collective-permute-start.37 = (bf16[1,16,128]{2,1,0:T(8,128)(2,1)S(1)}, bf16[1,16,128]{2,1,0:T(8,128)(2,1)S(1)}, u32[]{:S(2)}, u32[]{:S(2)}) collective-permute-start(bf16[1,16,128]{2,1,0:T(8,128)(2,1)S(1)} %constant_dynamic-slice_fusion.1), channel_id=1, source_target_pairs={{0,14},{2,0},{4,2},{6,4},{8,6},{10,8},{12,10},{14,12},{1,15},{3,1}... | collective-permute-start | bytes 12296 | tf_op jit(solution)/shard_map/ppermute | solution.py:24
  226.2 6.3 %collective-permute-start.39 = (bf16[1,16,128]{2,1,0:T(8,128)(2,1)S(1)}, bf16[1,16,128]{2,1,0:T(8,128)(2,1)S(1)}, u32[]{:S(2)}, u32[]{:S(2)}) collective-permute-start(bf16[1,16,128]{2,1,0:T(8,128)(2,1)S(1)} %collective-permute-done.38), channel_id=1, source_target_pairs={{0,14},{2,0},{4,2},{6,4},{8,6},{10,8},{12,10},{14,12},{1,15},{3,1}... | collective-permute-start | bytes 12296 | tf_op jit(solution)/shard_map/ppermute | solution.py:24
  232.5 6.3 %collective-permute-start.40 = (bf16[1,16,128]{2,1,0:T(8,128)(2,1)S(1)}, bf16[1,16,128]{2,1,0:T(8,128)(2,1)S(1)}, u32[]{:S(2)}, u32[]{:S(2)}) collective-permute-start(bf16[1,16,128]{2,1,0:T(8,128)(2,1)S(1)} %collective-permute-done.39), channel_id=1, source_target_pairs={{0,14},{2,0},{4,2},{6,4},{8,6},{10,8},{12,10},{14,12},{1,15},{3,1}... | collective-permute-start | bytes 12296 | tf_op jit(solution)/shard_map/ppermute | solution.py:24
  238.8 6.3 %collective-permute-start.41 = (bf16[1,16,128]{2,1,0:T(8,128)(2,1)S(1)}, bf16[1,16,128]{2,1,0:T(8,128)(2,1)S(1)}, u32[]{:S(2)}, u32[]{:S(2)}) collective-permute-start(bf16[1,16,128]{2,1,0:T(8,128)(2,1)S(1)} %collective-permute-done.40), channel_id=1, source_target_pairs={{0,14},{2,0},{4,2},{6,4},{8,6},{10,8},{12,10},{14,12},{1,15},{3,1}... | collective-permute-start | bytes 12296 | tf_op jit(solution)/shard_map/ppermute | solution.py:24
  245.1 6.3 %collective-permute-start.42 = (bf16[1,16,128]{2,1,0:T(8,128)(2,1)S(1)}, bf16[1,16,128]{2,1,0:T(8,128)(2,1)S(1)}, u32[]{:S(2)}, u32[]{:S(2)}) collective-permute-start(bf16[1,16,128]{2,1,0:T(8,128)(2,1)S(1)} %collective-permute-done.41), channel_id=1, source_target_pairs={{0,14},{2,0},{4,2},{6,4},{8,6},{10,8},{12,10},{14,12},{1,15},{3,1}... | collective-permute-start | bytes 12296 | tf_op jit(solution)/shard_map/ppermute | solution.py:24
  251.4 6.3 %collective-permute-start.43 = (bf16[1,16,128]{2,1,0:T(8,128)(2,1)S(1)}, bf16[1,16,128]{2,1,0:T(8,128)(2,1)S(1)}, u32[]{:S(2)}, u32[]{:S(2)}) collective-permute-start(bf16[1,16,128]{2,1,0:T(8,128)(2,1)S(1)} %collective-permute-done.42), channel_id=1, source_target_pairs={{0,14},{2,0},{4,2},{6,4},{8,6},{10,8},{12,10},{14,12},{1,15},{3,1}... | collective-permute-start | bytes 12296 | tf_op jit(solution)/shard_map/ppermute | solution.py:24
  (41 other events, 481.5 us)
